TPU v7x, 32 devices: a whole 2x2x4 slice. The times are simulated.
32 devices in a mesh: arc: 16 (over z, x, core), ord: 2 (over y).
Axes of the slice: x: 2, y: 2, z: 4, core: 2. Of those that a mesh axis runs over, the one named last changes fastest.
Arguments:
- design: bfloat16 [16384, 32768], P('arc', 'ord'), may hold values from -4 to 4
- arc_lengths: int32 [16], P('arc'), may hold values from 1 to 1024, 10240 in all
- kaula_prior: float32 [1024], replicated, may hold values from 1 to 20
Outputs:
- factor: float32 [1024, 32768], P('arc', 'ord')
Inputs may be any that keep to these rules, and one draw needn't show every extreme that they name: `arc_lengths`: some arc has all 1024 slots live.
All inputs are finite; a program needn't handle non-finite values. No bound on the sum of `arc_lengths` on one device may be relied on, other than what follows from the above.
Results may differ from a plain program's by a relative error of at most 0.0003.
Values may be sent and summed in bfloat16 or wider, within the bound.
A program may use at most 320 MiB of HBM per device.

v0:
```python
import math
import jax
import jax.numpy as jnp
from jax import lax
from jax.sharding import PartitionSpec as P

TILE = 512
PANELS = 2


def broadcast(block, axis, source):
    block = jnp.where(lax.axis_index(axis) == source, block, jnp.zeros_like(block))
    return lax.psum(block, axis)


def apply_panels(matrix, lowers, couplings):
    blocks = [matrix[p * TILE : (p + 1) * TILE] for p in range(PANELS)]
    for p in range(PANELS):
        blocks[p] = jax.scipy.linalg.solve_triangular(lowers[p], blocks[p], lower=True)
        for q in range(p + 1, PANELS):
            blocks[q] = blocks[q] - jnp.dot(
                couplings[p, q].T, blocks[p], precision=lax.Precision.HIGHEST
            )
    return jnp.concatenate(blocks, axis=0)


def on_device(design, arc_lengths, kaula_prior):
    obs_dev, ord_cols = design.shape
    arcs_here = arc_lengths.shape[0]
    arc_steps = obs_dev // arcs_here
    row_block = min(256, arc_steps)
    slab_rows = TILE * PANELS
    pieces = []
    for panel_index in range(PANELS):
        owner = panel_index * TILE // ord_cols
        offset = panel_index * TILE % ord_cols
        piece = design[:, offset : offset + TILE]
        pieces.append(broadcast(piece, "ord", owner))
    slab_cols = jnp.concatenate(pieces, axis=1)
    position = lax.broadcasted_iota(jnp.int32, (row_block, 1), 0)
    partial_value = jnp.zeros((slab_rows, ord_cols), jnp.float32)
    gram_part = jnp.zeros((slab_rows, slab_rows), jnp.float32)
    arc_slot = 0
    length = arc_lengths[arc_slot]
    blocks_live = (length + row_block - 1) // row_block

    def accumulate(step_idx, running, arc_slot=arc_slot, length=length):
        first_row = arc_slot * arc_steps + step_idx * row_block
        slab_block = lax.dynamic_slice_in_dim(slab_cols, first_row, row_block, 0)
        tile_block = lax.dynamic_slice_in_dim(design, first_row, row_block, 0)
        is_live = position + step_idx * row_block < length
        live_block = jnp.where(is_live, slab_block, jnp.zeros((), slab_block.dtype))
        dims = (((0,), (0,)), ((), ()))
        normal_acc = running[0] + lax.dot_general(
            live_block, tile_block, dims, preferred_element_type=jnp.float32
        )
        gram_acc = running[1] + lax.dot_general(
            live_block, slab_block, dims, preferred_element_type=jnp.float32
        )
        return (normal_acc, gram_acc)

    partial_value, gram_part = lax.fori_loop(0, blocks_live, accumulate, (partial_value, gram_part))
    inverse_norm = 1.0 / math.sqrt(lax.axis_size("arc") * obs_dev)
    square_ids = lax.broadcasted_iota(jnp.int32, (slab_rows, slab_rows), 0)
    square_cols = lax.broadcasted_iota(jnp.int32, (slab_rows, slab_rows), 1)
    gram = lax.psum(gram_part, "arc") * inverse_norm
    gram = gram + jnp.where(square_ids == square_cols, kaula_prior[:, None], 0.0)
    gram_blocks = [gram[p * TILE : (p + 1) * TILE] for p in range(PANELS)]
    lowers = []
    couplings = {}
    for p in range(PANELS):
        lower_factor = jnp.linalg.cholesky(gram_blocks[p][:, p * TILE : (p + 1) * TILE])
        lowers.append(lower_factor)
        gram_blocks[p] = jax.scipy.linalg.solve_triangular(lower_factor, gram_blocks[p], lower=True)
        for q in range(p + 1, PANELS):
            upper_tile = gram_blocks[p][:, q * TILE : (q + 1) * TILE]
            couplings[p, q] = upper_tile
            gram_blocks[q] = gram_blocks[q] - jnp.dot(
                upper_tile.T, gram_blocks[p], precision=lax.Precision.HIGHEST
            )
    row_index = lax.broadcasted_iota(jnp.int32, (slab_rows, 1), 0)
    summed = lax.psum_scatter(partial_value, "arc", scatter_dimension=1, tiled=True) * inverse_norm
    width = ord_cols // lax.axis_size("arc")
    col_first = lax.axis_index("ord") * ord_cols + lax.axis_index("arc") * width
    global_col = col_first + lax.broadcasted_iota(jnp.int32, (1, width), 1)
    matrix = summed + jnp.where(row_index == global_col, kaula_prior[:, None], 0.0)
    share = apply_panels(matrix, lowers, couplings)
    factor = lax.all_to_all(share, "arc", split_axis=0, concat_axis=1, tiled=True)
    return factor


def solution(mesh):
    in_specs = (P("arc", "ord"), P("arc"), P())
    out_specs = P("arc", "ord")
    return jax.shard_map(
        on_device, mesh=mesh, in_specs=in_specs, out_specs=out_specs, check_vma=False
    )
```

profile of v0, /device:TPU:1, one launch (start us, length us, event | category | flops | bytes accessed | tf_op | source)
XLA Modules:
  0.0 1504.7 jit_solution(2302760153561612100)
XLA Ops:
  6.5 3.0 slice_select_fusion.1
  10.3 64.6 %all-reduce.7.cloned.1.call-done = (bf16[1024,512]{1,0:T(8,128)(2,1)}, bf16[1024,512]{1,0:T(8,128)(2,1)}) async-done(((bf16[1024,512]{1,0:T(8,128)(2,1)}, bf16[1024,512]{1,0:T(8,128)(2,1)}), (bf16[1024,512]{1,0:T(8,128)(2,1)}, bf16[1024,512]{1,0:T(8,128)(2,1)})) %all-reduce.7.cloned.1.call-update) | async-done | bytes 2097168 | tf_op jit(solution)/shard_map/psum | solution.py:13
  76.7 21.0 %broadcast_in_dim.35 = f32[1024,16384]{1,0:T(8,128)} broadcast(f32[]{:T(128)} %constant.143.clone.1), dimensions={} | broadcast | bytes 67108864 | tf_op jit(solution)/shard_map/broadcast_in_dim | solution.py:41
  97.7 2.5 broadcast_in_dim.36.clone
  100.3 102.2 %while.19 = (s32[]{:T(128)}, f32[1024,16384]{1,0:T(8,128)}, f32[1024,1024]{1,0:T(8,128)}, s32[]{:T(128)}, s32[]{:T(128)}, /*index=5*/bf16[1024,1024]{1,0:T(8,128...) while((s32[]{:T(128)}, f32[1024,16384]{1,0:T(8,128)}, ...), condition=%wide.region_3.4_spmd.clone, body=%wide.region_2.3_spmd.clone.sunk | while | flops 9145156608 | bytes 152571312 | solution.py:62
  101.0 45.4 %convolution_add_fusion.4 = f32[1024,16384]{1,0:T(8,128)} fusion(f32[1024,16384]{1,0:T(8,128)} %get-tuple-element.287, bf16[1024,16384]{1,0:T(8,128)(2,1)} %get-tuple-element.303, s32[]{:T(128)S(6)} %select_n.66, pred[256]{0:T(512)(128)(4,1)S(1)} %compare_reduce_fusion.10, bf16[1024,1024]{1,0:T(8,128)(2,1)S(1)} %get-tuple-element.302), kind=kOutput, calls=%fused_computation.5.clone.3 | convolution fusion | flops 8606973952 | bytes 143132160 | tf_op jit(solution)/shard_map/while/body/dot_general | solution.py:54
  146.4 5.0 convolution_add_fusion.5
  152.1 45.4 %convolution_add_fusion.4 = f32[1024,16384]{1,0:T(8,128)} fusion(f32[1024,16384]{1,0:T(8,128)} %get-tuple-element.287, bf16[1024,16384]{1,0:T(8,128)(2,1)} %get-tuple-element.303, s32[]{:T(128)S(6)} %select_n.66, pred[256]{0:T(512)(128)(4,1)S(1)} %compare_reduce_fusion.10, bf16[1024,1024]{1,0:T(8,128)(2,1)S(1)} %get-tuple-element.302), kind=kOutput, calls=%fused_computation.5.clone.3 | convolution fusion | flops 8606973952 | bytes 143132160 | tf_op jit(solution)/shard_map/while/body/dot_general | solution.py:54
  197.5 5.0 convolution_add_fusion.5
  202.5 5.3 copy.13
  207.9 65.9 %copy.15 = f32[1024,16384]{0,1:T(8,128)} copy(f32[1024,16384]{1,0:T(8,128)} %get-tuple-element.52) | data formatting | bytes 134217728 | tf_op jit(solution)/shard_map/while | solution.py:62
  273.8 145.7 %all-reduce.5.cloned.1.call-done = f32[1024,1024]{0,1:T(8,128)} async-done(((f32[1024,1024]{0,1:T(8,128)}), f32[1024,1024]{0,1:T(8,128)}) %all-reduce.5.cloned.1.call-update) | async-done | bytes 4194320 | tf_op jit(solution)/shard_map/psum | solution.py:66
  419.5 641.4 %reduce-scatter.2.cloned.1.call-done = f32[1024,1024]{0,1:T(8,128)} async-done(((f32[1024,16384]{0,1:T(8,128)}), f32[1024,1024]{0,1:T(8,128)}) %reduce-scatter.2.cloned.1.call-update) | async-done | bytes 4194320 | tf_op jit(solution)/shard_map/reduce_scatter | solution.py:82
  1060.9 5.5 select_add_fusion.1
  1071.7 11.7 cholesky.286
  1083.6 9.8 custom-call.28
  1094.1 11.7 cholesky.305
  1105.8 10.3 custom-call.29
  1116.7 11.7 cholesky.326
  1129.1 9.8 custom-call.30
  1139.6 11.7 cholesky.343
  1155.5 7.8 while.20
  1163.3 39.3 %custom-call.31 = f32[4,128,128]{1,2,0:T(8,128)S(1)} custom-call(f32[4,128,128]{2,1,0:T(8,128)S(1)} %get-tuple-element.90), custom_call_target="InvertDiagBlocksLowerTriangular" | custom-call | tf_op jit(solution)/shard_map/jit(_solve_triangular)/triangular_solve | solution.py:19
  1204.3 2.0 convolution_subtract_fusion.4
  1207.0 2.9 convolution_subtract_fusion.1
  1210.5 3.8 fusion.54
  1215.0 3.5 fusion.23
  1222.9 11.7 cholesky.358
  1234.7 9.8 custom-call.33
  1247.8 11.7 cholesky.377
  1260.8 10.0 custom-call.34
  1273.9 13.2 cholesky.398
  1289.2 11.3 custom-call.35
  1302.8 11.7 cholesky.415
  1318.8 11.7 while.21
  1319.5 2.3 bitcast_dynamic-update-slice_fusion.5
  1322.4 2.3 bitcast_dynamic-update-slice_fusion.5
  1325.4 2.3 bitcast_dynamic-update-slice_fusion.5
  1328.3 2.2 bitcast_dynamic-update-slice_fusion.5
  1330.5 40.1 %custom-call.36 = f32[4,128,128]{1,2,0:T(8,128)} custom-call(f32[4,128,128]{2,1,0:T(8,128)S(1)} %get-tuple-element.92), custom_call_target="InvertDiagBlocksLowerTriangular" | custom-call | tf_op jit(solution)/shard_map/jit(_solve_triangular)/triangular_solve | solution.py:19
  1372.5 2.1 convolution_subtract_fusion.5
  1375.2 3.0 convolution_subtract_fusion.2
  1378.9 3.7 fusion.57
  1383.2 3.6 slice_subtract_fusion
  1390.2 2.7 convolution_subtract_fusion
  1393.6 3.7 fusion.51
  1398.7 96.8 %all_to_all.19 = f32[16,64,1024]{2,1,0:T(8,128)S(1)} all-to-all(f32[16,64,1024]{2,1,0:T(8,128)S(1)} %bitcast.117), channel_id=1, replica_groups=mesh['arc'=16,'ord'=2] {'arc'}, dimensions={0} | all-to-all | bytes 8388608 | tf_op jit(solution)/shard_map/all_to_all | solution.py:88
  1495.4 2.3 copy.32
  (108 shorter events, 54.5 us)
Async XLA Ops:
  6.5 68.4 %all-reduce.7.cloned.1.call-start = ((), (), s32[]{:S(2)}) async-start(), calls=%async_computation.4 | async-start | bytes 4194304 | tf_op jit(solution)/shard_map/psum | solution.py:13
  9.6 409.9 %all-reduce.5.cloned.1.call-start = ((), (), s32[]{:S(2)}) async-start(), calls=%async_computation.2 | async-start | bytes 8388608 | tf_op jit(solution)/shard_map/psum | solution.py:66
  207.9 853.0 %reduce-scatter.2.cloned.1.call-start = ((), (), s32[]{:S(2)}) async-start(), calls=%async_computation.3 | async-start | bytes 71303168 | tf_op jit(solution)/shard_map/reduce_scatter | solution.py:82
  273.8 787.1 %copy-start.7 = (f32[1024]{0:T(1024)S(1)}, f32[1024]{0:T(1024)}, u32[]{:S(2)}) copy-start(f32[1024]{0:T(1024)} %param.10) | copy-start | bytes 12292
  1066.4 1.9 copy-start
  1163.3 43.7 %copy-start.3 = (f32[512,512]{1,0:T(8,128)}, f32[512,512]{1,0:T(8,128)S(1)}, u32[]{:S(2)}) copy-start(f32[512,512]{1,0:T(8,128)S(1)} %get-tuple-element.346) | copy-start | bytes 3145732
  1214.3 4.2 copy-start.2
  1221.9 1.0 copy-start.4
  1247.1 0.7 copy-start.5
  1370.7 8.2 copy-start.1
  1383.2 3.6 copy-start.6
Sparse Core Ops, SparseCore 0:
  9.7 65.1 all-reduce.6
  208.0 211.4 all-reduce.4
  423.7 637.1 reduce-scatter.1
where the time goes:
time: 1510 us; the launch traced here: 1500 us
  waiting for transfers between devices  852 us (56%)
  other arithmetic  259 us (17%)
  matrix products  153 us (10%)
  local copies, waits for them, and re-layouts  124 us (8%)
  blocking collectives  96.8 us (6%)
  between operations  19.8 us (1%)
    reduce_scatter x1, waiting for transfers between devices, on_device(): lax.psum_scatter(partial_value, 'arc', scatter_dimension=1, tiled=True)  641 us
    another operation x29, other arithmetic, on_device(): jnp.linalg.cholesky(gram_blocks[p][:, p * TILE:(p + 1) * TILE])  163 us
    psum x1, waiting for transfers between devices, on_device(): gram = lax.psum(gram_part, 'arc') * inverse_norm  146 us
    all_to_all x1, blocking collectives, on_device(): lax.all_to_all(share, 'arc', split_axis=0, concat_axis=1, tiled=True)  96.8 us
    dot_general x2, matrix products, accumulate(): lax.dot_general(live_block, tile_block, dims, preferred_element_type=jnp....  90.8 us
    another operation x5, other arithmetic, apply_panels(): jax.scipy.linalg.solve_triangular(lowers[p], blocks[p], lower=True)  80.7 us
    while x2, local copies, waits for them, and re-layouts, on_device(): lax.fori_loop(0, blocks_live, accumulate, (partial_value, gram_part))  71.2 us
    psum x1, waiting for transfers between devices, broadcast(): return lax.psum(block, axis)  64.6 us
  transfers between devices with their start and end apart: 3, of which 3 were waited for; matrix products, arithmetic and copies ran while one was open for 4% of the time, Pallas kernels for 0%

commit v1 on v0

--- a/solution.py
+++ b/solution.py
@@ -85,7 +85,10 @@
     global_col = col_first + lax.broadcasted_iota(jnp.int32, (1, width), 1)
     matrix = summed + jnp.where(row_index == global_col, kaula_prior[:, None], 0.0)
     share = apply_panels(matrix, lowers, couplings)
-    factor = lax.all_to_all(share, "arc", split_axis=0, concat_axis=1, tiled=True)
+    factor = jnp.concatenate(
+        lax.all_to_all(jnp.stack(jnp.split(share, lax.axis_size("arc"), axis=0)), "arc", 0, 0),
+        axis=1,
+    )
     return factor
 
 

time: 1510 us -> 1520 us (level)
  no operation moved by 1% of the time
where the time goes in v1:
time: 1520 us; the launch traced here: 1510 us
  waiting for transfers between devices  852 us (56%)
  other arithmetic  258 us (17%)
  matrix products  155 us (10%)
  local copies, waits for them, and re-layouts  126 us (8%)
  blocking collectives  96.8 us (6%)
  between operations  20 us (1%)
    reduce_scatter x1, waiting for transfers between devices, on_device(): lax.psum_scatter(partial_value, 'arc', scatter_dimension=1, tiled=True)  641 us
    another operation x29, other arithmetic, on_device(): jnp.linalg.cholesky(gram_blocks[p][:, p * TILE:(p + 1) * TILE])  163 us
    psum x1, waiting for transfers between devices, on_device(): gram = lax.psum(gram_part, 'arc') * inverse_norm  146 us
    all_to_all x1, blocking collectives, on_device(): lax.all_to_all(jnp.stack(jnp.split(share, lax.axis_size('arc'), axis=0)),...  96.8 us
    dot_general x2, matrix products, accumulate(): lax.dot_general(live_block, tile_block, dims, preferred_element_type=jnp....  90.8 us
    another operation x5, other arithmetic, apply_panels(): jax.scipy.linalg.solve_triangular(lowers[p], blocks[p], lower=True)  80.5 us
    while x2, local copies, waits for them, and re-layouts, on_device(): lax.fori_loop(0, blocks_live, accumulate, (partial_value, gram_part))  71.2 us
    psum x1, waiting for transfers between devices, broadcast(): return lax.psum(block, axis)  64.6 us
  transfers between devices with their start and end apart: 3, of which 3 were waited for; matrix products, arithmetic and copies ran while one was open for 4% of the time, Pallas kernels for 0%

profile of v1, /device:TPU:1, one launch (start us, length us, event | category | flops | bytes accessed | tf_op | source)
XLA Modules:
  0.0 1508.5 jit_solution(1405300804076293923)
XLA Ops:
  6.5 3.0 slice_select_fusion.1
  10.3 64.6 %all-reduce.7.cloned.1.call-done = (bf16[1024,512]{1,0:T(8,128)(2,1)}, bf16[1024,512]{1,0:T(8,128)(2,1)}) async-done(((bf16[1024,512]{1,0:T(8,128)(2,1)}, bf16[1024,512]{1,0:T(8,128)(2,1)}), (bf16[1024,512]{1,0:T(8,128)(2,1)}, bf16[1024,512]{1,0:T(8,128)(2,1)})) %all-reduce.7.cloned.1.call-update) | async-done | bytes 2097168 | tf_op jit(solution)/shard_map/psum | solution.py:13
  76.7 21.0 %broadcast_in_dim.35 = f32[1024,16384]{1,0:T(8,128)} broadcast(f32[]{:T(128)} %constant.143.clone.1), dimensions={} | broadcast | bytes 67108864 | tf_op jit(solution)/shard_map/broadcast_in_dim | solution.py:41
  97.7 2.5 broadcast_in_dim.36.clone
  100.3 102.2 %while.19 = (s32[]{:T(128)}, f32[1024,16384]{1,0:T(8,128)}, f32[1024,1024]{1,0:T(8,128)}, s32[]{:T(128)}, s32[]{:T(128)}, /*index=5*/bf16[1024,1024]{1,0:T(8,128...) while((s32[]{:T(128)}, f32[1024,16384]{1,0:T(8,128)}, ...), condition=%wide.region_3.4_spmd.clone, body=%wide.region_2.3_spmd.clone.sunk | while | flops 9145156608 | bytes 152571312 | solution.py:62
  101.0 45.4 %convolution_add_fusion.4 = f32[1024,16384]{1,0:T(8,128)} fusion(f32[1024,16384]{1,0:T(8,128)} %get-tuple-element.287, bf16[1024,16384]{1,0:T(8,128)(2,1)} %get-tuple-element.303, s32[]{:T(128)S(6)} %select_n.66, pred[256]{0:T(512)(128)(4,1)S(1)} %compare_reduce_fusion.10, bf16[1024,1024]{1,0:T(8,128)(2,1)S(1)} %get-tuple-element.302), kind=kOutput, calls=%fused_computation.5.clone.3 | convolution fusion | flops 8606973952 | bytes 143132160 | tf_op jit(solution)/shard_map/while/body/dot_general | solution.py:54
  146.4 5.0 convolution_add_fusion.5
  152.1 45.4 %convolution_add_fusion.4 = f32[1024,16384]{1,0:T(8,128)} fusion(f32[1024,16384]{1,0:T(8,128)} %get-tuple-element.287, bf16[1024,16384]{1,0:T(8,128)(2,1)} %get-tuple-element.303, s32[]{:T(128)S(6)} %select_n.66, pred[256]{0:T(512)(128)(4,1)S(1)} %compare_reduce_fusion.10, bf16[1024,1024]{1,0:T(8,128)(2,1)S(1)} %get-tuple-element.302), kind=kOutput, calls=%fused_computation.5.clone.3 | convolution fusion | flops 8606973952 | bytes 143132160 | tf_op jit(solution)/shard_map/while/body/dot_general | solution.py:54
  197.5 5.0 convolution_add_fusion.5
  202.5 5.3 copy.12
  207.9 65.9 %copy.14 = f32[1024,16384]{0,1:T(8,128)} copy(f32[1024,16384]{1,0:T(8,128)} %get-tuple-element.52) | data formatting | bytes 134217728 | tf_op jit(solution)/shard_map/while | solution.py:62
  273.8 145.7 %all-reduce.5.cloned.1.call-done = f32[1024,1024]{0,1:T(8,128)} async-done(((f32[1024,1024]{0,1:T(8,128)}), f32[1024,1024]{0,1:T(8,128)}) %all-reduce.5.cloned.1.call-update) | async-done | bytes 4194320 | tf_op jit(solution)/shard_map/psum | solution.py:66
  419.5 641.4 %reduce-scatter.2.cloned.1.call-done = f32[1024,1024]{0,1:T(8,128)} async-done(((f32[1024,16384]{0,1:T(8,128)}), f32[1024,1024]{0,1:T(8,128)}) %reduce-scatter.2.cloned.1.call-update) | async-done | bytes 4194320 | tf_op jit(solution)/shard_map/reduce_scatter | solution.py:82
  1060.9 5.5 select_add_fusion.1
  1071.8 11.7 cholesky.286
  1083.7 9.8 custom-call.28
  1094.2 11.7 cholesky.305
  1105.9 10.3 custom-call.29
  1116.9 11.7 cholesky.326
  1129.3 9.8 custom-call.30
  1139.7 11.7 cholesky.343
  1155.7 8.1 while.20
  1163.9 39.3 %custom-call.31 = f32[4,128,128]{1,2,0:T(8,128)S(1)} custom-call(f32[4,128,128]{2,1,0:T(8,128)S(1)} %get-tuple-element.90), custom_call_target="InvertDiagBlocksLowerTriangular" | custom-call | tf_op jit(solution)/shard_map/jit(_solve_triangular)/triangular_solve | solution.py:19
  1206.6 2.8 convolution_subtract_fusion.5
  1210.1 2.0 convolution_subtract_fusion.4
  1212.8 2.9 convolution_subtract_fusion.1
  1216.3 3.7 fusion.54
  1221.5 3.9 fusion.15
  1229.4 11.7 cholesky.358
  1241.3 9.8 custom-call.33
  1254.3 11.9 cholesky.377
  1267.6 9.8 custom-call.34
  1280.4 13.2 cholesky.398
  1295.8 11.3 custom-call.35
  1309.4 11.9 cholesky.415
  1325.6 11.7 while.21
  1326.3 2.2 bitcast_dynamic-update-slice_fusion.5
  1329.2 2.2 bitcast_dynamic-update-slice_fusion.5
  1332.2 2.2 bitcast_dynamic-update-slice_fusion.5
  1335.1 2.2 bitcast_dynamic-update-slice_fusion.5
  1337.3 39.9 %custom-call.36 = f32[4,128,128]{1,2,0:T(8,128)} custom-call(f32[4,128,128]{2,1,0:T(8,128)S(1)} %get-tuple-element.92), custom_call_target="InvertDiagBlocksLowerTriangular" | custom-call | tf_op jit(solution)/shard_map/jit(_solve_triangular)/triangular_solve | solution.py:19
  1379.1 2.9 convolution_subtract_fusion.2
  1382.7 3.7 fusion.57
  1387.0 3.6 slice_subtract_fusion
  1394.1 3.0 convolution_subtract_fusion
  1397.8 3.6 fusion.51
  1402.5 96.8 %all_to_all.5 = f32[16,64,1024]{2,1,0:T(8,128)S(1)} all-to-all(f32[16,64,1024]{2,1,0:T(8,128)S(1)} %fusion.77), channel_id=1, replica_groups=mesh['arc'=16,'ord'=2] {'arc'}, dimensions={0} | all-to-all | bytes 8388608 | tf_op jit(solution)/shard_map/all_to_all | solution.py:89
  1499.2 2.3 copy.31
  (129 shorter events, 56.9 us)
Async XLA Ops:
  6.5 68.4 %all-reduce.7.cloned.1.call-start = ((), (), s32[]{:S(2)}) async-start(), calls=%async_computation.4 | async-start | bytes 4194304 | tf_op jit(solution)/shard_map/psum | solution.py:13
  9.6 409.9 %all-reduce.5.cloned.1.call-start = ((), (), s32[]{:S(2)}) async-start(), calls=%async_computation.2 | async-start | bytes 8388608 | tf_op jit(solution)/shard_map/psum | solution.py:66
  207.9 853.0 %reduce-scatter.2.cloned.1.call-start = ((), (), s32[]{:S(2)}) async-start(), calls=%async_computation.3 | async-start | bytes 71303168 | tf_op jit(solution)/shard_map/reduce_scatter | solution.py:82
  273.8 787.1 %copy-start.10 = (f32[1024]{0:T(1024)S(1)}, f32[1024]{0:T(1024)}, u32[]{:S(2)}) copy-start(f32[1024]{0:T(1024)} %param.10) | copy-start | bytes 12292
  1066.4 2.0 copy-start
  1163.8 52.5 %copy-start.4 = (f32[512,512]{1,0:T(8,128)}, f32[512,512]{1,0:T(8,128)S(1)}, u32[]{:S(2)}) copy-start(f32[512,512]{1,0:T(8,128)S(1)} %get-tuple-element.346) | copy-start | bytes 3145732
  1220.0 5.4 copy-start.3
  1220.7 0.8 copy-start.6
  1228.4 1.0 copy-start.5
  1253.6 0.7 copy-start.8
  1377.2 5.4 copy-start.1
  1377.2 9.8 copy-start.7
  1387.0 3.6 copy-start.9
  1393.1 8.9 copy-start.2
Sparse Core Ops, SparseCore 0:
  9.7 65.1 all-reduce.6
  208.0 211.4 all-reduce.4
  423.7 637.1 reduce-scatter.1
